TPU v7x, 32 devices: a whole 2x2x4 slice. The times are simulated.
32 devices in a mesh: seq: 8 (over z, core), dp: 4 (over y, x).
Axes of the slice: x: 2, y: 2, z: 4, core: 2. Of those that a mesh axis runs over, the one named last changes fastest.
Arguments:
- query_proj: bfloat16 [3072, 2560], P(('dp', 'seq')), parts along dimension 0, may hold values from -4.5 to 4.5
- key_proj: bfloat16 [3072, 2560], P(('dp', 'seq')), parts along dimension 0, may hold values from -4.5 to 4.5
- value_proj: bfloat16 [3072, 2560], P(('dp', 'seq')), parts along dimension 0, may hold values from -16 to 16
- token_rows: int32 [3072], P('dp'), parts along dimension 0, may hold values from 0 to 767, as said below
- key_tiles: int32 [64, 4], P(('dp', 'seq')), parts along dimension 0, may hold values from 0 to 15, as said below
- key_count: int32 [64], P(('dp', 'seq')), parts along dimension 0, may hold values from 1 to 4
Outputs:
- attended: bfloat16 [3072, 2560], P(('dp', 'seq')), parts along dimension 0
There are 4 independent parts, one for each index of `dp`. A program takes and returns all parts, laid end to end along the dimension named above; each array names one. Nothing has to cross between parts.
Inputs may be any that keep to these rules, and one draw needn't show every extreme that they name: token_rows is a permutation; the rows of every aligned block of 96 frame-slab rows go to every aligned block of 96 tile-order rows exactly 96 // 8 times. `key_tiles`: for query tile i the entries m < key_count[i] are distinct, include i, and each lies between 2 * (i // 2 - 2) and 2 * (i // 2 + 2) + 1; later entries equal i.
All inputs are finite; a program needn't handle non-finite values.
Results may differ from a plain program's by a relative error of at most 0.0049.
Values may be sent and summed in bfloat16 or wider, within the bound.
No kernel may reach another device: no remote copies, remote signals or barrier semaphores. Data moves between devices by JAX's collectives and lax.ppermute only.
A program may use at most 64 MiB of HBM per device.

v0:
```python
import jax
import jax.numpy as jnp
from jax import lax
from jax.sharding import PartitionSpec as P

HD = 128
KMAX = 4
REACH = 2


def passed_along(value, axis, by):
    size = lax.axis_size(axis)
    pairs = [(i, i + by) for i in range(size) if 0 <= i + by < size]
    return lax.ppermute(value, axis, pairs)


def order_for(inverse, owner_dev, rows_dev):
    sources = lax.dynamic_slice_in_dim(inverse, owner_dev * rows_dev, rows_dev) // rows_dev
    keyed = sources * rows_dev + jnp.arange(rows_dev, dtype=jnp.int32)
    return jnp.argsort(keyed)


def attend_heads(query_rows, key_rows, value_rows, allowed, head_count):
    last = query_rows.ndim - 1

    def one_head(head_index):
        start = head_index * HD
        query_head = lax.dynamic_slice_in_dim(query_rows, start, HD, last)
        key_head = lax.dynamic_slice_in_dim(key_rows, start, HD, last)
        value_head = lax.dynamic_slice_in_dim(value_rows, start, HD, last)
        scores = jnp.einsum(
            "...qd,...kd->...qk", query_head, key_head, preferred_element_type=jnp.float32
        ) * HD ** (-0.5)
        scores = jnp.where(allowed, scores, -jnp.inf)
        peak = jnp.max(scores, axis=-1, keepdims=True)
        exponent = jnp.exp(scores - peak)
        weights = (exponent / jnp.sum(exponent, axis=-1, keepdims=True)).astype(jnp.bfloat16)
        mixed = jnp.einsum(
            "...qk,...kd->...qd", weights, value_head, preferred_element_type=jnp.float32
        )
        return mixed.astype(jnp.bfloat16)

    return lax.map(one_head, jnp.arange(head_count))


def shards(query_proj, key_proj, value_proj, token_rows, key_tiles, key_count):
    members = lax.axis_size("seq")
    myself = lax.axis_index("seq")
    rows_dev = query_proj.shape[0]
    feat_width = query_proj.shape[1]
    per_peer = rows_dev // members
    tile_rows = rows_dev // 2
    head_count = feat_width // HD
    inverse = jnp.argsort(token_rows)
    own_dest = lax.dynamic_slice_in_dim(token_rows, myself * rows_dev, rows_dev)
    send_order = jnp.argsort(own_dest)
    sorted_query = query_proj[send_order].reshape(members, per_peer, feat_width)
    sorted_keys = key_proj[send_order].reshape(members, per_peer, feat_width)
    sorted_values = value_proj[send_order].reshape(members, per_peer, feat_width)
    order_own = order_for(inverse, myself, rows_dev)
    placement_own = jnp.argsort(order_own)
    arrived_query, arrived_keys, arrived_values = (
        lax.all_to_all(sorted_query, "seq", split_axis=0, concat_axis=0, tiled=True),
        lax.all_to_all(sorted_keys, "seq", split_axis=0, concat_axis=0, tiled=True),
        lax.all_to_all(sorted_values, "seq", split_axis=0, concat_axis=0, tiled=True),
    )
    query_tile = arrived_query.reshape(rows_dev, feat_width)[placement_own]
    key_tile = arrived_keys.reshape(rows_dev, feat_width)[placement_own]
    value_tile = arrived_values.reshape(rows_dev, feat_width)[placement_own]
    blocks = []
    for offset in range(-REACH, REACH + 1):
        if offset == 0:
            blocks.append((key_tile, value_tile))
        else:
            blocks.append(passed_along((key_tile, value_tile), "seq", -offset))
    window_keys = jnp.concatenate([pair[0] for pair in blocks], axis=0)
    window_values = jnp.concatenate([pair[1] for pair in blocks], axis=0)
    entry_live = jnp.arange(KMAX)[None, :] < key_count[:, None]
    window_ids = (
        (myself + jnp.arange(-REACH, REACH + 1))[:, None] * 2 + jnp.arange(2)[None, :]
    ).reshape(-1)
    matches = (key_tiles[:, :, None] == window_ids[None, None, :]) & entry_live[:, :, None]
    listed = jnp.any(matches, axis=1)
    allowed = jnp.repeat(jnp.repeat(listed, tile_rows, axis=0), tile_rows, axis=1)
    mixed = attend_heads(query_tile, window_keys, window_values, allowed, head_count)
    tile_out = jnp.moveaxis(mixed, 0, -2).reshape(rows_dev, feat_width)
    back_send = tile_out[order_own].reshape(members, per_peer, feat_width)
    arrived_back = lax.all_to_all(back_send, "seq", split_axis=0, concat_axis=0, tiled=True)
    return arrived_back.reshape(rows_dev, feat_width)[jnp.argsort(send_order)]


def solution(mesh):
    return jax.shard_map(
        shards,
        mesh=mesh,
        in_specs=(
            P(("dp", "seq"), None),
            P(("dp", "seq"), None),
            P(("dp", "seq"), None),
            P("dp"),
            P(("dp", "seq"), None),
            P(("dp", "seq")),
        ),
        out_specs=P(("dp", "seq"), None),
        check_vma=False,
    )
```

profile of v0, /device:TPU:0, one launch (start us, length us, event | category | flops | bytes accessed | tf_op | source)
XLA Modules:
  0.0 226.7 jit_solution(4143252565832732605)
XLA Ops:
  0.0 5.1 %sort.77 = (s32[768]{0:T(1024)}, s32[768]{0:T(1024)S(1)}) sort(s32[768]{0:T(1024)} %param.11, s32[768]{0:T(1024)S(1)} %iota.41), dimensions={0}, to_apply=%region_1.2 | sort | flops 7680 | bytes 12288 | tf_op jit(solution)/shard_map/jit(argsort)/sort | solution.py:54
  6.0 2.5 %sort.78 = (s32[96]{0:T(128)}, s32[96]{0:T(128)S(1)}) sort(s32[96]{0:T(128)S(1)} %iota_add_fusion.1, s32[96]{0:T(128)S(1)} %iota.43), dimensions={0}, to_apply=%region_2.3 | sort | flops 672 | bytes 1536 | tf_op jit(solution)/shard_map/jit(argsort)/sort | solution.py:20
  8.5 2.5 %sort.76 = (s32[96]{0:T(128)}, s32[96]{0:T(128)S(1)}) sort(s32[96]{0:T(128)S(1)} %dynamic_slice.19, s32[96]{0:T(128)S(1)} %iota.40), dimensions={0}, to_apply=%region_0.0 | sort | flops 672 | bytes 1536 | tf_op jit(solution)/shard_map/jit(argsort)/sort | solution.py:56
  12.9 6.4 %all-to-all-start.2 = ((bf16[8,12,2560]{2,1,0:T(8,128)(2,1)}), bf16[8,12,2560]{2,1,0:T(8,128)(2,1)S(1)}, u32[]{:S(2)}, u32[]{:S(2)}) async-start(bf16[8,12,2560]{2,1,0:T(8,128)(2,1)} %reshape.86), calls=%async_computation.2 | async-start | bytes 1310720 | tf_op jit(solution)/shard_map/all_to_all | solution.py:65
  21.1 16.3 %all-to-all-done.2 = bf16[8,12,2560]{2,1,0:T(8,128)(2,1)S(1)} async-done(((bf16[8,12,2560]{2,1,0:T(8,128)(2,1)}), bf16[8,12,2560]{2,1,0:T(8,128)(2,1)S(1)}, u32[]{:S(2)}, u32[]{:S(2)}) %all-to-all-start.2) | async-done | bytes 491552 | tf_op jit(solution)/shard_map/all_to_all | solution.py:65
  37.4 3.5 %all-to-all-start.1 = ((bf16[8,12,2560]{2,1,0:T(8,128)(2,1)}), bf16[8,12,2560]{2,1,0:T(8,128)(2,1)S(1)}, u32[]{:S(2)}, u32[]{:S(2)}) async-start(bf16[8,12,2560]{2,1,0:T(8,128)(2,1)} %reshape.82), calls=%async_computation.1 | async-start | bytes 1310720 | tf_op jit(solution)/shard_map/all_to_all | solution.py:64
  40.9 2.5 %sort.79 = (s32[96]{0:T(128)}, s32[96]{0:T(128)S(1)}) sort(s32[96]{0:T(128)S(1)} %get-tuple-element.49, s32[96]{0:T(128)S(1)} %iota.44), dimensions={0}, to_apply=%region_3.4 | sort | flops 672 | bytes 1536 | tf_op jit(solution)/shard_map/jit(argsort)/sort | solution.py:61
  45.3 13.7 %all-to-all-done.1 = bf16[8,12,2560]{2,1,0:T(8,128)(2,1)S(1)} async-done(((bf16[8,12,2560]{2,1,0:T(8,128)(2,1)}), bf16[8,12,2560]{2,1,0:T(8,128)(2,1)S(1)}, u32[]{:S(2)}, u32[]{:S(2)}) %all-to-all-start.1) | async-done | bytes 491552 | tf_op jit(solution)/shard_map/all_to_all | solution.py:64
  59.0 3.5 %all-to-all-start = ((bf16[8,12,2560]{2,1,0:T(8,128)(2,1)}), bf16[8,12,2560]{2,1,0:T(8,128)(2,1)S(1)}, u32[]{:S(2)}, u32[]{:S(2)}) async-start(bf16[8,12,2560]{2,1,0:T(8,128)(2,1)} %reshape.80), calls=%async_computation | async-start | bytes 1310720 | tf_op jit(solution)/shard_map/all_to_all | solution.py:63
  63.6 4.6 %collective-permute-start.4 = (bf16[96,2560]{1,0:T(8,128)(2,1)S(1)}, bf16[96,2560]{1,0:T(8,128)(2,1)}, u32[]{:S(2)}, u32[]{:S(2)}) collective-permute-start(bf16[96,2560]{1,0:T(8,128)(2,1)S(1)} %gather_fusion.5), channel_id=1, source_target_pairs={{0,8},{4,12},{8,16},{12,20},{16,24},{20,28},{1,9},{5,13},{9,17},{1... | collective-permute-start | bytes 1474568 | tf_op jit(solution)/shard_map/ppermute | solution.py:14
  68.3 2.5 %collective-permute-start.5 = (bf16[96,2560]{1,0:T(8,128)(2,1)S(1)}, bf16[96,2560]{1,0:T(8,128)(2,1)}, u32[]{:S(2)}, u32[]{:S(2)}) collective-permute-start(bf16[96,2560]{1,0:T(8,128)(2,1)S(1)} %gather_fusion.5), channel_id=1, source_target_pairs={{0,4},{4,8},{8,12},{12,16},{16,20},{20,24},{24,28},{1,5},{5,9},{9,... | collective-permute-start | bytes 1474568 | tf_op jit(solution)/shard_map/ppermute | solution.py:14
  71.3 1.3 collective-permute-start.6
  72.6 1.3 collective-permute-start.7
  74.9 5.8 %collective-permute-start = (bf16[96,2560]{1,0:T(8,128)(2,1)S(1)}, bf16[96,2560]{1,0:T(8,128)(2,1)}, u32[]{:S(2)}, u32[]{:S(2)}) collective-permute-start(bf16[96,2560]{1,0:T(8,128)(2,1)S(1)} %gather_fusion.3), channel_id=1, source_target_pairs={{0,8},{4,12},{8,16},{12,20},{16,24},{20,28},{1,9},{5,13},{9,17},{1... | collective-permute-start | bytes 1474568 | tf_op jit(solution)/shard_map/ppermute | solution.py:14
  82.2 2.7 %collective-permute-done.4 = bf16[96,2560]{1,0:T(8,128)(2,1)} collective-permute-done((bf16[96,2560]{1,0:T(8,128)(2,1)S(1)}, bf16[96,2560]{1,0:T(8,128)(2,1)}, u32[]{:S(2)}, u32[]{:S(2)}) %collective-permute-start.4) | collective-permute-done | bytes 491552 | tf_op jit(solution)/shard_map/ppermute | solution.py:14
  84.9 1.6 collective-permute-start.1
  86.5 1.8 constant_dynamic-update-slice_fusion.9
  88.4 1.3 collective-permute-start.2
  89.6 1.9 constant_dynamic-update-slice_fusion.8
  92.3 3.1 %collective-permute-done = bf16[96,2560]{1,0:T(8,128)(2,1)} collective-permute-done((bf16[96,2560]{1,0:T(8,128)(2,1)S(1)}, bf16[96,2560]{1,0:T(8,128)(2,1)}, u32[]{:S(2)}, u32[]{:S(2)}) %collective-permute-start) | collective-permute-done | bytes 491552 | tf_op jit(solution)/shard_map/ppermute | solution.py:14
  95.5 1.3 collective-permute-start.3
  97.9 1.9 constant_dynamic-update-slice_fusion.6
  99.8 1.9 constant_dynamic-update-slice_fusion.5
  101.7 13.1 %collective-permute-done.3 = bf16[96,2560]{1,0:T(8,128)(2,1)S(1)} collective-permute-done((bf16[96,2560]{1,0:T(8,128)(2,1)S(1)}, bf16[96,2560]{1,0:T(8,128)(2,1)S(1)}, u32[]{:S(2)}, u32[]{:S(2)}) %collective-permute-start.3) | collective-permute-done | bytes 491552 | tf_op jit(solution)/shard_map/ppermute | solution.py:14
  114.8 1.4 copy-done.3
  116.3 79.9 %while.11 = (s32[]{:T(128)}, bf16[20,96,128]{2,1,0:T(8,128)(2,1)S(1)}, s32[20]{0:T(128)S(1)}, bf16[96,2560]{1,0:T(8,128)(2,1)S(1)}, bf16[480,2560]{1,0:T(8,128)(...) while((s32[]{:T(128)}, ...), condition=%wide.region_8.9_spmd.clone, body=%wide.region_5.8_spmd.clone.sunk | while | flops 23973700 | bytes 1052395 | solution.py:43
  117.7 1.2 fusion.20
  121.7 1.2 fusion.20
  123.1 1.2 fusion.22
  125.7 1.2 fusion.20
  127.1 1.2 fusion.22
  129.7 1.2 fusion.20
  131.1 1.2 fusion.22
  133.7 1.2 fusion.20
  137.7 1.2 fusion.20
  139.1 1.2 fusion.22
  141.7 1.2 fusion.20
  143.1 1.2 fusion.22
  145.7 1.2 fusion.20
  147.1 1.2 fusion.22
  149.7 1.2 fusion.20
  153.7 1.2 fusion.20
  155.1 1.2 fusion.22
  157.6 1.2 fusion.20
  159.1 1.2 fusion.22
  161.6 1.2 fusion.20
  163.1 1.2 fusion.22
  165.6 1.2 fusion.20
  169.6 1.2 fusion.20
  171.1 1.2 fusion.22
  173.6 1.2 fusion.20
  175.1 1.2 fusion.22
  177.6 1.2 fusion.20
  179.1 1.2 fusion.22
  181.6 1.2 fusion.20
  185.6 1.2 fusion.20
  187.0 1.2 fusion.22
  189.6 1.2 fusion.20
  191.0 1.2 fusion.22
  193.6 1.2 fusion.20
  198.1 8.8 %all-to-all-start.3 = ((bf16[8,12,2560]{2,1,0:T(8,128)(2,1)}), bf16[8,12,2560]{2,1,0:T(8,128)(2,1)S(1)}, u32[]{:S(2)}, u32[]{:S(2)}) async-start(bf16[8,12,2560]{2,1,0:T(8,128)(2,1)} %reshape.89), calls=%async_computation.3 | async-start | bytes 1310720 | tf_op jit(solution)/shard_map/all_to_all | solution.py:88
  206.8 2.5 %sort.80 = (s32[96]{0:T(128)}, s32[96]{0:T(128)S(1)}) sort(s32[96]{0:T(128)S(1)} %get-tuple-element.47, s32[96]{0:T(128)S(1)} %iota.46), dimensions={0}, to_apply=%region_9.10 | sort | flops 672 | bytes 1536 | tf_op jit(solution)/shard_map/jit(argsort)/sort | solution.py:89
  209.4 15.6 %all-to-all-done.3 = bf16[8,12,2560]{2,1,0:T(8,128)(2,1)S(1)} async-done(((bf16[8,12,2560]{2,1,0:T(8,128)(2,1)}), bf16[8,12,2560]{2,1,0:T(8,128)(2,1)S(1)}, u32[]{:S(2)}, u32[]{:S(2)}) %all-to-all-start.3) | async-done | bytes 491552 | tf_op jit(solution)/shard_map/all_to_all | solution.py:88
  225.1 1.6 gather_fusion.7
  (151 shorter events, 40.1 us)
Async XLA Ops:
  0.0 11.1 %copy-start = (bf16[96,2560]{1,0:T(8,128)(2,1)S(1)}, bf16[96,2560]{1,0:T(8,128)(2,1)}, u32[]{:S(2)}) copy-start(bf16[96,2560]{1,0:T(8,128)(2,1)} %param.10) | copy-start | bytes 1474564
  11.1 8.2 %copy-start.1 = (bf16[96,2560]{1,0:T(8,128)(2,1)S(1)}, bf16[96,2560]{1,0:T(8,128)(2,1)}, u32[]{:S(2)}) copy-start(bf16[96,2560]{1,0:T(8,128)(2,1)} %param.9) | copy-start | bytes 1474564
  12.9 24.5 %all-to-all-start.2 = ((bf16[8,12,2560]{2,1,0:T(8,128)(2,1)}), bf16[8,12,2560]{2,1,0:T(8,128)(2,1)S(1)}, u32[]{:S(2)}, u32[]{:S(2)}) async-start(bf16[8,12,2560]{2,1,0:T(8,128)(2,1)} %reshape.86), calls=%async_computation.2 | async-start | bytes 1310720 | tf_op jit(solution)/shard_map/all_to_all | solution.py:65
  19.3 24.2 %copy-start.2 = (bf16[96,2560]{1,0:T(8,128)(2,1)S(1)}, bf16[96,2560]{1,0:T(8,128)(2,1)}, u32[]{:S(2)}) copy-start(bf16[96,2560]{1,0:T(8,128)(2,1)} %param.8) | copy-start | bytes 1474564
  37.4 21.6 %all-to-all-start.1 = ((bf16[8,12,2560]{2,1,0:T(8,128)(2,1)}), bf16[8,12,2560]{2,1,0:T(8,128)(2,1)S(1)}, u32[]{:S(2)}, u32[]{:S(2)}) async-start(bf16[8,12,2560]{2,1,0:T(8,128)(2,1)} %reshape.82), calls=%async_computation.1 | async-start | bytes 1310720 | tf_op jit(solution)/shard_map/all_to_all | solution.py:64
  59.0 22.2 %all-to-all-start = ((bf16[8,12,2560]{2,1,0:T(8,128)(2,1)}), bf16[8,12,2560]{2,1,0:T(8,128)(2,1)S(1)}, u32[]{:S(2)}, u32[]{:S(2)}) async-start(bf16[8,12,2560]{2,1,0:T(8,128)(2,1)} %reshape.80), calls=%async_computation | async-start | bytes 1310720 | tf_op jit(solution)/shard_map/all_to_all | solution.py:63
  62.7 8.1 %copy-start.6 = (s32[2]{0:T(128)S(1)}, s32[2]{0:T(128)}, u32[]{:S(2)}) copy-start(s32[2]{0:T(128)} %param.13) | copy-start | bytes 28
  62.7 8.2 %copy-start.5 = (s32[2,4]{1,0:T(2,128)S(1)}, s32[2,4]{1,0:T(2,128)}, u32[]{:S(2)}) copy-start(s32[2,4]{1,0:T(2,128)} %param.12) | copy-start | bytes 100
  63.6 21.3 %collective-permute-start.4 = (bf16[96,2560]{1,0:T(8,128)(2,1)S(1)}, bf16[96,2560]{1,0:T(8,128)(2,1)}, u32[]{:S(2)}, u32[]{:S(2)}) collective-permute-start(bf16[96,2560]{1,0:T(8,128)(2,1)S(1)} %gather_fusion.5), channel_id=1, source_target_pairs={{0,8},{4,12},{8,16},{12,20},{16,24},{20,28},{1,9},{5,13},{9,17},{1... | collective-permute-start | bytes 1474568 | tf_op jit(solution)/shard_map/ppermute | solution.py:14
  68.3 20.1 %collective-permute-start.5 = (bf16[96,2560]{1,0:T(8,128)(2,1)S(1)}, bf16[96,2560]{1,0:T(8,128)(2,1)}, u32[]{:S(2)}, u32[]{:S(2)}) collective-permute-start(bf16[96,2560]{1,0:T(8,128)(2,1)S(1)} %gather_fusion.5), channel_id=1, source_target_pairs={{0,4},{4,8},{8,12},{12,16},{16,20},{20,24},{24,28},{1,5},{5,9},{9,... | collective-permute-start | bytes 1474568 | tf_op jit(solution)/shard_map/ppermute | solution.py:14
  71.3 26.6 %collective-permute-start.6 = (bf16[96,2560]{1,0:T(8,128)(2,1)S(1)}, bf16[96,2560]{1,0:T(8,128)(2,1)}, u32[]{:S(2)}, u32[]{:S(2)}) collective-permute-start(bf16[96,2560]{1,0:T(8,128)(2,1)S(1)} %gather_fusion.5), channel_id=1, source_target_pairs={{4,0},{8,4},{12,8},{16,12},{20,16},{24,20},{28,24},{5,1},{9,5},{13... | collective-permute-start | bytes 1474568 | tf_op jit(solution)/shard_map/ppermute | solution.py:14
  72.6 27.2 %collective-permute-start.7 = (bf16[96,2560]{1,0:T(8,128)(2,1)S(1)}, bf16[96,2560]{1,0:T(8,128)(2,1)}, u32[]{:S(2)}, u32[]{:S(2)}) collective-permute-start(bf16[96,2560]{1,0:T(8,128)(2,1)S(1)} %gather_fusion.5), channel_id=1, source_target_pairs={{8,0},{12,4},{16,8},{20,12},{24,16},{28,20},{9,1},{13,5},{17,9},{2... | collective-permute-start | bytes 1474568 | tf_op jit(solution)/shard_map/ppermute | solution.py:14
  74.9 20.6 %collective-permute-start = (bf16[96,2560]{1,0:T(8,128)(2,1)S(1)}, bf16[96,2560]{1,0:T(8,128)(2,1)}, u32[]{:S(2)}, u32[]{:S(2)}) collective-permute-start(bf16[96,2560]{1,0:T(8,128)(2,1)S(1)} %gather_fusion.3), channel_id=1, source_target_pairs={{0,8},{4,12},{8,16},{12,20},{16,24},{20,28},{1,9},{5,13},{9,17},{1... | collective-permute-start | bytes 1474568 | tf_op jit(solution)/shard_map/ppermute | solution.py:14
  84.9 12.9 %collective-permute-start.1 = (bf16[96,2560]{1,0:T(8,128)(2,1)S(1)}, bf16[96,2560]{1,0:T(8,128)(2,1)S(1)}, u32[]{:S(2)}, u32[]{:S(2)}) collective-permute-start(bf16[96,2560]{1,0:T(8,128)(2,1)S(1)} %gather_fusion.3), channel_id=1, source_target_pairs={{0,4},{4,8},{8,12},{12,16},{16,20},{20,24},{24,28},{1,5},{5,9},{9,... | collective-permute-start | bytes 1474568 | tf_op jit(solution)/shard_map/ppermute | solution.py:14
  88.4 13.3 %collective-permute-start.2 = (bf16[96,2560]{1,0:T(8,128)(2,1)S(1)}, bf16[96,2560]{1,0:T(8,128)(2,1)S(1)}, u32[]{:S(2)}, u32[]{:S(2)}) collective-permute-start(bf16[96,2560]{1,0:T(8,128)(2,1)S(1)} %gather_fusion.3), channel_id=1, source_target_pairs={{4,0},{8,4},{12,8},{16,12},{20,16},{24,20},{28,24},{5,1},{9,5},{13... | collective-permute-start | bytes 1474568 | tf_op jit(solution)/shard_map/ppermute | solution.py:14
  95.5 19.3 %collective-permute-start.3 = (bf16[96,2560]{1,0:T(8,128)(2,1)S(1)}, bf16[96,2560]{1,0:T(8,128)(2,1)S(1)}, u32[]{:S(2)}, u32[]{:S(2)}) collective-permute-start(bf16[96,2560]{1,0:T(8,128)(2,1)S(1)} %gather_fusion.3), channel_id=1, source_target_pairs={{8,0},{12,4},{16,8},{20,12},{24,16},{28,20},{9,1},{13,5},{17,9},{2... | collective-permute-start | bytes 1474568 | tf_op jit(solution)/shard_map/ppermute | solution.py:14
  97.9 18.4 %copy-start.4 = (bf16[20,96,128]{2,1,0:T(8,128)(2,1)S(1)}, bf16[20,96,128]{2,1,0:T(8,128)(2,1)}, u32[]{:S(2)}) copy-start(bf16[20,96,128]{2,1,0:T(8,128)(2,1)} %custom-call.18) | copy-start | bytes 1474564
  114.8 1.4 copy-start.3
  198.1 26.9 %all-to-all-start.3 = ((bf16[8,12,2560]{2,1,0:T(8,128)(2,1)}), bf16[8,12,2560]{2,1,0:T(8,128)(2,1)S(1)}, u32[]{:S(2)}, u32[]{:S(2)}) async-start(bf16[8,12,2560]{2,1,0:T(8,128)(2,1)} %reshape.89), calls=%async_computation.3 | async-start | bytes 1310720 | tf_op jit(solution)/shard_map/all_to_all | solution.py:88
where the time goes:
time: 229 us; the launch traced here: 227 us
  waiting for transfers between devices  65 us (28%)
  matrix products  47.2 us (21%)
  starting transfers between devices  41.8 us (18%)
  local copies, waits for them, and re-layouts  38.8 us (17%)
  other arithmetic  19.6 us (9%)
  loops' own time  14 us (6%)
    dot_general x20, matrix products, one_head(): jnp.einsum('...qd,...kd->...qk', query_head, key_head, preferred_element_...  24.2 us
    dot_general x20, matrix products, one_head(): jnp.einsum('...qk,...kd->...qd', weights, value_head, preferred_element_t...  23 us
    ppermute x8, starting transfers between devices, passed_along(): return lax.ppermute(value, axis, pairs)  19.6 us
    ppermute x8, waiting for transfers between devices, passed_along(): return lax.ppermute(value, axis, pairs)  18.9 us
    all_to_all x1, waiting for transfers between devices, shards(): lax.all_to_all(sorted_values, 'seq', split_axis=0, concat_axis=0, tiled=T...  16.3 us
    all_to_all x1, waiting for transfers between devices, shards(): lax.all_to_all(back_send, 'seq', split_axis=0, concat_axis=0, tiled=True)  15.6 us
    another operation x1, loops' own time, attend_heads(): return lax.map(one_head, jnp.arange(head_count))  14 us
    all_to_all x1, waiting for transfers between devices, shards(): lax.all_to_all(sorted_keys, 'seq', split_axis=0, concat_axis=0, tiled=True)  13.7 us
  transfers between devices with their start and end apart: 12, of which 7 were waited for; matrix products, arithmetic and copies ran while one was open for 10% of the time, Pallas kernels for 0%

commit v1 on v0

--- a/solution.py
+++ b/solution.py
@@ -6,6 +6,28 @@
 HD = 128
 KMAX = 4
 REACH = 2
+
+
+def split_up(x, dim, size):
+    before, after = (x.shape[:dim], x.shape[dim + 1 :])
+    return jnp.moveaxis(x.reshape(*before, size, -1, *after), dim, 0)
+
+
+def in_order(blocks, dim):
+    blocks = jnp.moveaxis(blocks, 0, dim)
+    dims = blocks.shape
+    return blocks.reshape(*dims[:dim], dims[dim] * dims[dim + 1], *dims[dim + 2 :])
+
+
+def pairwise_exchange(shard, axis, split_dim, concat_dim):
+    size, index = (lax.axis_size(axis), lax.axis_index(axis))
+    blocks = split_up(shard, split_dim, size)
+    outs = [blocks[index]]
+    for step in range(1, size):
+        sent = blocks[index ^ step]
+        outs.append(lax.ppermute(sent, axis, [(i, i ^ step) for i in range(size)]))
+    blocks = jnp.stack(outs)[index ^ jnp.arange(size)]
+    return in_order(blocks, concat_dim)
 
 
 def passed_along(value, axis, by):
@@ -62,7 +84,7 @@
     arrived_query, arrived_keys, arrived_values = (
         lax.all_to_all(sorted_query, "seq", split_axis=0, concat_axis=0, tiled=True),
         lax.all_to_all(sorted_keys, "seq", split_axis=0, concat_axis=0, tiled=True),
-        lax.all_to_all(sorted_values, "seq", split_axis=0, concat_axis=0, tiled=True),
+        pairwise_exchange(sorted_values, "seq", 0, 0),
     )
     query_tile = arrived_query.reshape(rows_dev, feat_width)[placement_own]
     key_tile = arrived_keys.reshape(rows_dev, feat_width)[placement_own]

time: 229 us -> 220 us (0.961)
  waiting for transfers between devices: 65 us -> 47.4 us
  starting transfers between devices: 41.8 us -> 49.5 us
    all_to_all x1 -> x0, waiting for transfers between devices: 16.3 us -> none  [shards(): lax.all_to_all(sorted_values, 'seq', split_axis=0, concat_axis=0, tiled=T...]
    all_to_all x1, waiting for transfers between devices: 13.7 us -> 0.01 us  [shards(): lax.all_to_all(sorted_keys, 'seq', split_axis=0, concat_axis=0, tiled=True)]
    ppermute x0 -> x7, waiting for transfers between devices: none -> 11.9 us  [pairwise_exchange(): outs.append(lax.ppermute(sent, axis, [(i, i ^ step) for i in range(size)]))]
    ppermute x0 -> x7, starting transfers between devices: none -> 9.94 us  [pairwise_exchange(): outs.append(lax.ppermute(sent, axis, [(i, i ^ step) for i in range(size)]))]
    all_to_all x1 -> x0, starting transfers between devices: 6.35 us -> none  [shards(): lax.all_to_all(sorted_values, 'seq', split_axis=0, concat_axis=0, tiled=T...]
    all_to_all x1, starting transfers between devices: 8.77 us -> 3.91 us  [shards(): lax.all_to_all(back_send, 'seq', split_axis=0, concat_axis=0, tiled=True)]
    all_to_all x1, starting transfers between devices: 3.54 us -> 7.81 us  [shards(): lax.all_to_all(sorted_query, 'seq', split_axis=0, concat_axis=0, tiled=True)]
    ppermute x8, starting transfers between devices: 19.6 us -> 22.9 us  [passed_along(): return lax.ppermute(value, axis, pairs)]
  transfers between devices with their start and end apart: 12 -> 18, of which waited for: 7 -> 7; matrix products, arithmetic and copies ran while one was open for 10% -> 10% of each run, Pallas kernels for 0% -> 0%
where the time goes in v1:
time: 220 us; the launch traced here: 218 us
  starting transfers between devices  49.5 us (22%)
  waiting for transfers between devices  47.4 us (22%)
  matrix products  47.2 us (21%)
  local copies, waits for them, and re-layouts  39.7 us (18%)
  other arithmetic  19.6 us (9%)
  loops' own time  14 us (6%)
    dot_general x20, matrix products, one_head(): jnp.einsum('...qd,...kd->...qk', query_head, key_head, preferred_element_...  24.2 us
    dot_general x20, matrix products, one_head(): jnp.einsum('...qk,...kd->...qd', weights, value_head, preferred_element_t...  23 us
    ppermute x8, starting transfers between devices, passed_along(): return lax.ppermute(value, axis, pairs)  22.9 us
    ppermute x8, waiting for transfers between devices, passed_along(): return lax.ppermute(value, axis, pairs)  16.4 us
    all_to_all x1, waiting for transfers between devices, shards(): lax.all_to_all(back_send, 'seq', split_axis=0, concat_axis=0, tiled=True)  15.6 us
    another operation x1, loops' own time, attend_heads(): return lax.map(one_head, jnp.arange(head_count))  14 us
    ppermute x7, waiting for transfers between devices, pairwise_exchange(): outs.append(lax.ppermute(sent, axis, [(i, i ^ step) for i in range(size)]))  11.9 us
    dynamic_slice x20, local copies, waits for them, and re-layouts, attend_heads(): return lax.map(one_head, jnp.arange(head_count))  11.7 us
  transfers between devices with their start and end apart: 18, of which 7 were waited for; matrix products, arithmetic and copies ran while one was open for 10% of the time, Pallas kernels for 0%

profile of v1, /device:TPU:0, one launch (start us, length us, event | category | flops | bytes accessed | tf_op | source)
XLA Modules:
  0.0 217.8 jit_solution(1596254357552877411)
XLA Ops:
  0.0 5.1 %sort.77 = (s32[768]{0:T(1024)}, s32[768]{0:T(1024)S(1)}) sort(s32[768]{0:T(1024)} %param.11, s32[768]{0:T(1024)S(1)} %iota.45), dimensions={0}, to_apply=%region_1.2 | sort | flops 7680 | bytes 12288 | tf_op jit(solution)/shard_map/jit(argsort)/sort | solution.py:76
  6.0 2.5 %sort.78 = (s32[96]{0:T(128)}, s32[96]{0:T(128)S(1)}) sort(s32[96]{0:T(128)S(1)} %iota_add_fusion.1, s32[96]{0:T(128)S(1)} %iota.47), dimensions={0}, to_apply=%region_2.3 | sort | flops 672 | bytes 1536 | tf_op jit(solution)/shard_map/jit(argsort)/sort | solution.py:42
  8.5 2.5 %sort.76 = (s32[96]{0:T(128)}, s32[96]{0:T(128)S(1)}) sort(s32[96]{0:T(128)S(1)} %dynamic_slice.43, s32[96]{0:T(128)S(1)} %iota.44), dimensions={0}, to_apply=%region_0.0 | sort | flops 672 | bytes 1536 | tf_op jit(solution)/shard_map/jit(argsort)/sort | solution.py:78
  12.7 2.6 %collective-permute-start.5 = (bf16[1,12,2560]{2,1,0:T(8,128)(2,1)S(1)}, bf16[1,12,2560]{2,1,0:T(8,128)(2,1)S(1)}, u32[]{:S(2)}, u32[]{:S(2)}) collective-permute-start(bf16[1,12,2560]{2,1,0:T(8,128)(2,1)S(1)} %get-tuple-element.91), channel_id=1, source_target_pairs={{0,8},{4,12},{8,0},{12,4},{16,24},{20,28},{24,16},{28,20},{1,9},{5... | collective-permute-start | bytes 184328 | tf_op jit(solution)/shard_map/ppermute | solution.py:28
  15.4 2.8 %collective-permute-start.7 = (bf16[1,12,2560]{2,1,0:T(8,128)(2,1)S(1)}, bf16[1,12,2560]{2,1,0:T(8,128)(2,1)S(1)}, u32[]{:S(2)}, u32[]{:S(2)}) collective-permute-start(bf16[1,12,2560]{2,1,0:T(8,128)(2,1)S(1)} %get-tuple-element.89), channel_id=1, source_target_pairs={{0,16},{4,20},{8,24},{12,28},{16,0},{20,4},{24,8},{28,12},{1,17},{... | collective-permute-start | bytes 184328 | tf_op jit(solution)/shard_map/ppermute | solution.py:28
  20.0 4.9 %all-to-all-start.1 = ((bf16[8,12,2560]{2,1,0:T(8,128)(2,1)}), bf16[8,12,2560]{2,1,0:T(8,128)(2,1)S(1)}, u32[]{:S(2)}, u32[]{:S(2)}) async-start(bf16[8,12,2560]{2,1,0:T(8,128)(2,1)} %reshape.92), calls=%async_computation.1 | async-start | bytes 1310720 | tf_op jit(solution)/shard_map/all_to_all | solution.py:86
  24.9 2.5 %sort.79 = (s32[96]{0:T(128)}, s32[96]{0:T(128)S(1)}) sort(s32[96]{0:T(128)S(1)} %get-tuple-element.49, s32[96]{0:T(128)S(1)} %iota.48), dimensions={0}, to_apply=%region_3.4 | sort | flops 672 | bytes 1536 | tf_op jit(solution)/shard_map/jit(argsort)/sort | solution.py:83
  27.5 3.9 %collective-permute-start.9 = (bf16[1,12,2560]{2,1,0:T(8,128)(2,1)S(1)}, bf16[1,12,2560]{2,1,0:T(8,128)(2,1)S(1)}, u32[]{:S(2)}, u32[]{:S(2)}) collective-permute-start(bf16[1,12,2560]{2,1,0:T(8,128)(2,1)S(1)} %get-tuple-element.87), channel_id=1, source_target_pairs={{0,24},{4,28},{8,16},{12,20},{16,8},{20,12},{24,0},{28,4},{1,25},{... | collective-permute-start | bytes 184328 | tf_op jit(solution)/shard_map/ppermute | solution.py:28
  31.6 11.3 %collective-permute-done.9 = bf16[1,12,2560]{2,1,0:T(8,128)(2,1)S(1)} collective-permute-done((bf16[1,12,2560]{2,1,0:T(8,128)(2,1)S(1)}, bf16[1,12,2560]{2,1,0:T(8,128)(2,1)S(1)}, u32[]{:S(2)}, u32[]{:S(2)}) %collective-permute-start.9) | collective-permute-done | bytes 61472 | tf_op jit(solution)/shard_map/ppermute | solution.py:28
  45.2 8.5 %collective-permute-start.11 = (bf16[96,2560]{1,0:T(8,128)(2,1)S(1)}, bf16[96,2560]{1,0:T(8,128)(2,1)S(1)}, u32[]{:S(2)}, u32[]{:S(2)}) collective-permute-start(bf16[96,2560]{1,0:T(8,128)(2,1)S(1)} %gather_fusion.6), channel_id=1, source_target_pairs={{0,8},{4,12},{8,16},{12,20},{16,24},{20,28},{1,9},{5,13},{9,17},{1... | collective-permute-start | bytes 1474568 | tf_op jit(solution)/shard_map/ppermute | solution.py:36
  53.9 2.8 %collective-permute-start.12 = (bf16[96,2560]{1,0:T(8,128)(2,1)S(1)}, bf16[96,2560]{1,0:T(8,128)(2,1)}, u32[]{:S(2)}, u32[]{:S(2)}) collective-permute-start(bf16[96,2560]{1,0:T(8,128)(2,1)S(1)} %gather_fusion.6), channel_id=1, source_target_pairs={{0,4},{4,8},{8,12},{12,16},{16,20},{20,24},{24,28},{1,5},{5,9},{9,... | collective-permute-start | bytes 1474568 | tf_op jit(solution)/shard_map/ppermute | solution.py:36
  58.9 1.3 collective-permute-start.13
  60.2 1.3 collective-permute-start.14
  61.5 3.7 %collective-permute-done.11 = bf16[96,2560]{1,0:T(8,128)(2,1)S(1)} collective-permute-done((bf16[96,2560]{1,0:T(8,128)(2,1)S(1)}, bf16[96,2560]{1,0:T(8,128)(2,1)S(1)}, u32[]{:S(2)}, u32[]{:S(2)}) %collective-permute-start.11) | collective-permute-done | bytes 491552 | tf_op jit(solution)/shard_map/ppermute | solution.py:36
  66.0 1.8 constant_dynamic-update-slice_fusion.8
  67.9 7.8 %all-to-all-start = ((bf16[8,12,2560]{2,1,0:T(8,128)(2,1)}), bf16[8,12,2560]{2,1,0:T(8,128)(2,1)S(1)}, u32[]{:S(2)}, u32[]{:S(2)}) async-start(bf16[8,12,2560]{2,1,0:T(8,128)(2,1)} %reshape.90), calls=%async_computation | async-start | bytes 1310720 | tf_op jit(solution)/shard_map/all_to_all | solution.py:85
  77.5 4.1 %collective-permute-start = (bf16[96,2560]{1,0:T(8,128)(2,1)S(1)}, bf16[96,2560]{1,0:T(8,128)(2,1)S(1)}, u32[]{:S(2)}, u32[]{:S(2)}) collective-permute-start(bf16[96,2560]{1,0:T(8,128)(2,1)S(1)} %gather_fusion.3), channel_id=1, source_target_pairs={{0,8},{4,12},{8,16},{12,20},{16,24},{20,28},{1,9},{5,13},{9,17},{1... | collective-permute-start | bytes 1474568 | tf_op jit(solution)/shard_map/ppermute | solution.py:36
  81.6 1.8 constant_dynamic-update-slice_fusion.6
  83.4 2.4 %collective-permute-start.1 = (bf16[96,2560]{1,0:T(8,128)(2,1)S(1)}, bf16[96,2560]{1,0:T(8,128)(2,1)}, u32[]{:S(2)}, u32[]{:S(2)}) collective-permute-start(bf16[96,2560]{1,0:T(8,128)(2,1)S(1)} %gather_fusion.3), channel_id=1, source_target_pairs={{0,4},{4,8},{8,12},{12,16},{16,20},{20,24},{24,28},{1,5},{5,9},{9,... | collective-permute-start | bytes 1474568 | tf_op jit(solution)/shard_map/ppermute | solution.py:36
  85.8 1.9 constant_dynamic-update-slice_fusion.5
  87.7 1.3 collective-permute-start.2
  89.0 1.3 collective-permute-start.3
  90.3 3.5 %all-to-all-done = bf16[8,12,2560]{2,1,0:T(8,128)(2,1)S(1)} async-done(((bf16[8,12,2560]{2,1,0:T(8,128)(2,1)}), bf16[8,12,2560]{2,1,0:T(8,128)(2,1)S(1)}, u32[]{:S(2)}, u32[]{:S(2)}) %all-to-all-start) | async-done | bytes 491552 | tf_op jit(solution)/shard_map/all_to_all | solution.py:85
  94.8 3.2 %collective-permute-done = bf16[96,2560]{1,0:T(8,128)(2,1)S(1)} collective-permute-done((bf16[96,2560]{1,0:T(8,128)(2,1)S(1)}, bf16[96,2560]{1,0:T(8,128)(2,1)S(1)}, u32[]{:S(2)}, u32[]{:S(2)}) %collective-permute-start) | collective-permute-done | bytes 491552 | tf_op jit(solution)/shard_map/ppermute | solution.py:36
  100.3 9.4 %collective-permute-done.3 = bf16[96,2560]{1,0:T(8,128)(2,1)} collective-permute-done((bf16[96,2560]{1,0:T(8,128)(2,1)S(1)}, bf16[96,2560]{1,0:T(8,128)(2,1)}, u32[]{:S(2)}, u32[]{:S(2)}) %collective-permute-start.3) | collective-permute-done | bytes 491552 | tf_op jit(solution)/shard_map/ppermute | solution.py:36
  110.8 1.4 copy-done.3
  112.2 79.9 %while.11 = (s32[]{:T(128)}, bf16[20,96,128]{2,1,0:T(8,128)(2,1)S(1)}, s32[20]{0:T(128)S(1)}, bf16[96,2560]{1,0:T(8,128)(2,1)S(1)}, bf16[480,2560]{1,0:T(8,128)(...) while((s32[]{:T(128)}, ...), condition=%wide.region_8.9_spmd.clone, body=%wide.region_5.8_spmd.clone.sunk | while | flops 23973700 | bytes 1052395 | solution.py:65
  113.6 1.2 fusion.21
  115.0 1.2 fusion.23
  117.6 1.2 fusion.21
  121.6 1.2 fusion.21
  123.0 1.2 fusion.23
  125.6 1.2 fusion.21
  129.6 1.2 fusion.21
  131.0 1.2 fusion.23
  133.6 1.2 fusion.21
  137.6 1.2 fusion.21
  139.0 1.2 fusion.23
  141.6 1.2 fusion.21
  145.6 1.2 fusion.21
  147.0 1.2 fusion.23
  149.6 1.2 fusion.21
  151.0 1.2 fusion.23
  153.6 1.2 fusion.21
  155.0 1.2 fusion.23
  157.6 1.2 fusion.21
  161.6 1.2 fusion.21
  163.0 1.2 fusion.23
  165.6 1.2 fusion.21
  167.0 1.2 fusion.23
  169.6 1.2 fusion.21
  171.0 1.2 fusion.23
  173.6 1.2 fusion.21
  177.6 1.2 fusion.21
  179.0 1.2 fusion.23
  181.6 1.2 fusion.21
  183.0 1.2 fusion.23
  185.6 1.2 fusion.21
  187.0 1.2 fusion.23
  189.6 1.2 fusion.21
  194.0 3.9 %all-to-all-start.2 = ((bf16[8,12,2560]{2,1,0:T(8,128)(2,1)}), bf16[8,12,2560]{2,1,0:T(8,128)(2,1)S(1)}, u32[]{:S(2)}, u32[]{:S(2)}) async-start(bf16[8,12,2560]{2,1,0:T(8,128)(2,1)} %reshape.97), calls=%async_computation.2 | async-start | bytes 1310720 | tf_op jit(solution)/shard_map/all_to_all | solution.py:110
  197.9 2.5 %sort.80 = (s32[96]{0:T(128)}, s32[96]{0:T(128)S(1)}) sort(s32[96]{0:T(128)S(1)} %get-tuple-element.47, s32[96]{0:T(128)S(1)} %iota.51), dimensions={0}, to_apply=%region_9.10 | sort | flops 672 | bytes 1536 | tf_op jit(solution)/shard_map/jit(argsort)/sort | solution.py:111
  200.5 15.6 %all-to-all-done.2 = bf16[8,12,2560]{2,1,0:T(8,128)(2,1)S(1)} async-done(((bf16[8,12,2560]{2,1,0:T(8,128)(2,1)}), bf16[8,12,2560]{2,1,0:T(8,128)(2,1)S(1)}, u32[]{:S(2)}, u32[]{:S(2)}) %all-to-all-start.2) | async-done | bytes 491552 | tf_op jit(solution)/shard_map/all_to_all | solution.py:110
  216.2 1.6 gather_fusion.8
  (174 shorter events, 44.8 us)
Async XLA Ops:
  0.0 11.1 %copy-start = (bf16[96,2560]{1,0:T(8,128)(2,1)S(1)}, bf16[96,2560]{1,0:T(8,128)(2,1)}, u32[]{:S(2)}) copy-start(bf16[96,2560]{1,0:T(8,128)(2,1)} %param.10) | copy-start | bytes 1474564
  11.1 7.1 %copy-start.1 = (bf16[96,2560]{1,0:T(8,128)(2,1)S(1)}, bf16[96,2560]{1,0:T(8,128)(2,1)}, u32[]{:S(2)}) copy-start(bf16[96,2560]{1,0:T(8,128)(2,1)} %param.9) | copy-start | bytes 1474564
  12.2 15.3 %collective-permute-start.4 = (bf16[1,12,2560]{2,1,0:T(8,128)(2,1)S(1)}, bf16[1,12,2560]{2,1,0:T(8,128)(2,1)S(1)}, u32[]{:S(2)}, u32[]{:S(2)}) collective-permute-start(bf16[1,12,2560]{2,1,0:T(8,128)(2,1)S(1)} %get-tuple-element.92), channel_id=1, source_target_pairs={{0,4},{4,0},{8,12},{12,8},{16,20},{20,16},{24,28},{28,24},{1,5},{5... | collective-permute-start | bytes 184328 | tf_op jit(solution)/shard_map/ppermute | solution.py:28
  12.7 18.7 %collective-permute-start.5 = (bf16[1,12,2560]{2,1,0:T(8,128)(2,1)S(1)}, bf16[1,12,2560]{2,1,0:T(8,128)(2,1)S(1)}, u32[]{:S(2)}, u32[]{:S(2)}) collective-permute-start(bf16[1,12,2560]{2,1,0:T(8,128)(2,1)S(1)} %get-tuple-element.91), channel_id=1, source_target_pairs={{0,8},{4,12},{8,0},{12,4},{16,24},{20,28},{24,16},{28,20},{1,9},{5... | collective-permute-start | bytes 184328 | tf_op jit(solution)/shard_map/ppermute | solution.py:28
  15.4 16.1 %collective-permute-start.6 = (bf16[1,12,2560]{2,1,0:T(8,128)(2,1)S(1)}, bf16[1,12,2560]{2,1,0:T(8,128)(2,1)S(1)}, u32[]{:S(2)}, u32[]{:S(2)}) collective-permute-start(bf16[1,12,2560]{2,1,0:T(8,128)(2,1)S(1)} %get-tuple-element.90), channel_id=1, source_target_pairs={{0,12},{4,8},{8,4},{12,0},{16,28},{20,24},{24,20},{28,16},{1,13},{... | collective-permute-start | bytes 184328 | tf_op jit(solution)/shard_map/ppermute | solution.py:28
  15.4 16.1 %collective-permute-start.7 = (bf16[1,12,2560]{2,1,0:T(8,128)(2,1)S(1)}, bf16[1,12,2560]{2,1,0:T(8,128)(2,1)S(1)}, u32[]{:S(2)}, u32[]{:S(2)}) collective-permute-start(bf16[1,12,2560]{2,1,0:T(8,128)(2,1)S(1)} %get-tuple-element.89), channel_id=1, source_target_pairs={{0,16},{4,20},{8,24},{12,28},{16,0},{20,4},{24,8},{28,12},{1,17},{... | collective-permute-start | bytes 184328 | tf_op jit(solution)/shard_map/ppermute | solution.py:28
  18.2 13.4 %collective-permute-start.8 = (bf16[1,12,2560]{2,1,0:T(8,128)(2,1)S(1)}, bf16[1,12,2560]{2,1,0:T(8,128)(2,1)S(1)}, u32[]{:S(2)}, u32[]{:S(2)}) collective-permute-start(bf16[1,12,2560]{2,1,0:T(8,128)(2,1)S(1)} %get-tuple-element.88), channel_id=1, source_target_pairs={{0,20},{4,16},{8,28},{12,24},{16,4},{20,0},{24,12},{28,8},{1,21},{... | collective-permute-start | bytes 184328 | tf_op jit(solution)/shard_map/ppermute | solution.py:28
  20.0 47.9 %all-to-all-start.1 = ((bf16[8,12,2560]{2,1,0:T(8,128)(2,1)}), bf16[8,12,2560]{2,1,0:T(8,128)(2,1)S(1)}, u32[]{:S(2)}, u32[]{:S(2)}) async-start(bf16[8,12,2560]{2,1,0:T(8,128)(2,1)} %reshape.92), calls=%async_computation.1 | async-start | bytes 1310720 | tf_op jit(solution)/shard_map/all_to_all | solution.py:86
  27.5 15.4 %collective-permute-start.9 = (bf16[1,12,2560]{2,1,0:T(8,128)(2,1)S(1)}, bf16[1,12,2560]{2,1,0:T(8,128)(2,1)S(1)}, u32[]{:S(2)}, u32[]{:S(2)}) collective-permute-start(bf16[1,12,2560]{2,1,0:T(8,128)(2,1)S(1)} %get-tuple-element.87), channel_id=1, source_target_pairs={{0,24},{4,28},{8,16},{12,20},{16,8},{20,12},{24,0},{28,4},{1,25},{... | collective-permute-start | bytes 184328 | tf_op jit(solution)/shard_map/ppermute | solution.py:28
  31.4 12.1 %collective-permute-start.10 = (bf16[1,12,2560]{2,1,0:T(8,128)(2,1)S(1)}, bf16[1,12,2560]{2,1,0:T(8,128)(2,1)S(1)}, u32[]{:S(2)}, u32[]{:S(2)}) collective-permute-start(bf16[1,12,2560]{2,1,0:T(8,128)(2,1)S(1)} %get-tuple-element.86), channel_id=1, source_target_pairs={{0,28},{4,24},{8,20},{12,16},{16,12},{20,8},{24,4},{28,0},{1,29},{... | collective-permute-start | bytes 184328 | tf_op jit(solution)/shard_map/ppermute | solution.py:28
  44.2 9.5 %copy-start.6 = (s32[2]{0:T(128)S(1)}, s32[2]{0:T(128)}, u32[]{:S(2)}) copy-start(s32[2]{0:T(128)} %param.13) | copy-start | bytes 28
  44.3 12.4 %copy-start.5 = (s32[2,4]{1,0:T(2,128)S(1)}, s32[2,4]{1,0:T(2,128)}, u32[]{:S(2)}) copy-start(s32[2,4]{1,0:T(2,128)} %param.12) | copy-start | bytes 100
  44.3 12.5 %copy-start.2 = (bf16[96,2560]{1,0:T(8,128)(2,1)S(1)}, bf16[96,2560]{1,0:T(8,128)(2,1)}, u32[]{:S(2)}) copy-start(bf16[96,2560]{1,0:T(8,128)(2,1)} %param.8) | copy-start | bytes 1474564
  45.2 20.0 %collective-permute-start.11 = (bf16[96,2560]{1,0:T(8,128)(2,1)S(1)}, bf16[96,2560]{1,0:T(8,128)(2,1)S(1)}, u32[]{:S(2)}, u32[]{:S(2)}) collective-permute-start(bf16[96,2560]{1,0:T(8,128)(2,1)S(1)} %gather_fusion.6), channel_id=1, source_target_pairs={{0,8},{4,12},{8,16},{12,20},{16,24},{20,28},{1,9},{5,13},{9,17},{1... | collective-permute-start | bytes 1474568 | tf_op jit(solution)/shard_map/ppermute | solution.py:36
  53.9 12.2 %collective-permute-start.12 = (bf16[96,2560]{1,0:T(8,128)(2,1)S(1)}, bf16[96,2560]{1,0:T(8,128)(2,1)}, u32[]{:S(2)}, u32[]{:S(2)}) collective-permute-start(bf16[96,2560]{1,0:T(8,128)(2,1)S(1)} %gather_fusion.6), channel_id=1, source_target_pairs={{0,4},{4,8},{8,12},{12,16},{16,20},{20,24},{24,28},{1,5},{5,9},{9,... | collective-permute-start | bytes 1474568 | tf_op jit(solution)/shard_map/ppermute | solution.py:36
  58.9 22.7 %collective-permute-start.13 = (bf16[96,2560]{1,0:T(8,128)(2,1)S(1)}, bf16[96,2560]{1,0:T(8,128)(2,1)}, u32[]{:S(2)}, u32[]{:S(2)}) collective-permute-start(bf16[96,2560]{1,0:T(8,128)(2,1)S(1)} %gather_fusion.6), channel_id=1, source_target_pairs={{4,0},{8,4},{12,8},{16,12},{20,16},{24,20},{28,24},{5,1},{9,5},{13... | collective-permute-start | bytes 1474568 | tf_op jit(solution)/shard_map/ppermute | solution.py:36
  60.2 25.6 %collective-permute-start.14 = (bf16[96,2560]{1,0:T(8,128)(2,1)S(1)}, bf16[96,2560]{1,0:T(8,128)(2,1)}, u32[]{:S(2)}, u32[]{:S(2)}) collective-permute-start(bf16[96,2560]{1,0:T(8,128)(2,1)S(1)} %gather_fusion.6), channel_id=1, source_target_pairs={{8,0},{12,4},{16,8},{20,12},{24,16},{28,20},{9,1},{13,5},{17,9},{2... | collective-permute-start | bytes 1474568 | tf_op jit(solution)/shard_map/ppermute | solution.py:36
  67.9 26.0 %all-to-all-start = ((bf16[8,12,2560]{2,1,0:T(8,128)(2,1)}), bf16[8,12,2560]{2,1,0:T(8,128)(2,1)S(1)}, u32[]{:S(2)}, u32[]{:S(2)}) async-start(bf16[8,12,2560]{2,1,0:T(8,128)(2,1)} %reshape.90), calls=%async_computation | async-start | bytes 1310720 | tf_op jit(solution)/shard_map/all_to_all | solution.py:85
  77.5 20.6 %collective-permute-start = (bf16[96,2560]{1,0:T(8,128)(2,1)S(1)}, bf16[96,2560]{1,0:T(8,128)(2,1)S(1)}, u32[]{:S(2)}, u32[]{:S(2)}) collective-permute-start(bf16[96,2560]{1,0:T(8,128)(2,1)S(1)} %gather_fusion.3), channel_id=1, source_target_pairs={{0,8},{4,12},{8,16},{12,20},{16,24},{20,28},{1,9},{5,13},{9,17},{1... | collective-permute-start | bytes 1474568 | tf_op jit(solution)/shard_map/ppermute | solution.py:36
  83.4 14.7 %collective-permute-start.1 = (bf16[96,2560]{1,0:T(8,128)(2,1)S(1)}, bf16[96,2560]{1,0:T(8,128)(2,1)}, u32[]{:S(2)}, u32[]{:S(2)}) collective-permute-start(bf16[96,2560]{1,0:T(8,128)(2,1)S(1)} %gather_fusion.3), channel_id=1, source_target_pairs={{0,4},{4,8},{8,12},{12,16},{16,20},{20,24},{24,28},{1,5},{5,9},{9,... | collective-permute-start | bytes 1474568 | tf_op jit(solution)/shard_map/ppermute | solution.py:36
  87.7 11.5 %collective-permute-start.2 = (bf16[96,2560]{1,0:T(8,128)(2,1)S(1)}, bf16[96,2560]{1,0:T(8,128)(2,1)}, u32[]{:S(2)}, u32[]{:S(2)}) collective-permute-start(bf16[96,2560]{1,0:T(8,128)(2,1)S(1)} %gather_fusion.3), channel_id=1, source_target_pairs={{4,0},{8,4},{12,8},{16,12},{20,16},{24,20},{28,24},{5,1},{9,5},{13... | collective-permute-start | bytes 1474568 | tf_op jit(solution)/shard_map/ppermute | solution.py:36
  89.0 20.7 %collective-permute-start.3 = (bf16[96,2560]{1,0:T(8,128)(2,1)S(1)}, bf16[96,2560]{1,0:T(8,128)(2,1)}, u32[]{:S(2)}, u32[]{:S(2)}) collective-permute-start(bf16[96,2560]{1,0:T(8,128)(2,1)S(1)} %gather_fusion.3), channel_id=1, source_target_pairs={{8,0},{12,4},{16,8},{20,12},{24,16},{28,20},{9,1},{13,5},{17,9},{2... | collective-permute-start | bytes 1474568 | tf_op jit(solution)/shard_map/ppermute | solution.py:36
  94.8 17.4 %copy-start.4 = (bf16[20,96,128]{2,1,0:T(8,128)(2,1)S(1)}, bf16[20,96,128]{2,1,0:T(8,128)(2,1)}, u32[]{:S(2)}) copy-start(bf16[20,96,128]{2,1,0:T(8,128)(2,1)} %custom-call.21) | copy-start | bytes 1474564
  110.8 1.4 copy-start.3
  194.0 22.0 %all-to-all-start.2 = ((bf16[8,12,2560]{2,1,0:T(8,128)(2,1)}), bf16[8,12,2560]{2,1,0:T(8,128)(2,1)S(1)}, u32[]{:S(2)}, u32[]{:S(2)}) async-start(bf16[8,12,2560]{2,1,0:T(8,128)(2,1)} %reshape.97), calls=%async_computation.2 | async-start | bytes 1310720 | tf_op jit(solution)/shard_map/all_to_all | solution.py:110
